TPU v7x, 32 devices: a whole 2x2x4 slice. The times are simulated.
32 devices in a mesh: row: 4 (over z), col: 8 (over y, x, core).
Axes of the slice: x: 2, y: 2, z: 4, core: 2. Of those that a mesh axis runs over, the one named last changes fastest.
Arguments:
- tokens: bfloat16 [256, 8192], P('col', 'row'), may hold values from -6 to 6
- out_grad: bfloat16 [256, 8192], P('col', 'row'), may hold values from -1.1953125 to 1.1953125
- w_gate: bfloat16 [8192, 16384], P('row', 'col'), may hold values from -0.0625 to 0.0625
- w_up: bfloat16 [8192, 16384], P('row', 'col'), may hold values from -0.0625 to 0.0625
- w_down: bfloat16 [16384, 8192], P('col', 'row'), may hold values from -0.046875 to 0.046875
Outputs:
- grad_input: bfloat16 [256, 8192], P('col', 'row')
- grad_gate: bfloat16 [8192, 16384], P('row', 'col')
- grad_up: bfloat16 [8192, 16384], P('row', 'col')
- grad_down: bfloat16 [16384, 8192], P('col', 'row')
All inputs are finite; a program needn't handle non-finite values.
Results may differ from a plain program's by a relative error of at most 0.0049.
Values may be sent and summed in bfloat16 or wider, within the bound.
A program may use at most 128 MiB of HBM per device.

v0:
```python
import jax
import jax.numpy as jnp
from jax import lax
from jax.sharding import PartitionSpec as P


def contract(left_array, right_array, left_dim, right_dim):
    return lax.dot_general(
        left_array,
        right_array,
        (((left_dim,), (right_dim,)), ((), ())),
        preferred_element_type=jnp.float32,
    )


def swiglu_back(gate_sum, up_sum, hidden_grad):
    logistic = jax.nn.sigmoid(gate_sum)
    active = gate_sum * logistic
    hidden = (active * up_sum).astype(jnp.bfloat16)
    up_grad = (hidden_grad * active).astype(jnp.bfloat16)
    gate_grad = (hidden_grad * up_sum * logistic * (1.0 + gate_sum * (1.0 - logistic))).astype(
        jnp.bfloat16
    )
    return (hidden, gate_grad, up_grad)


def shards(tokens, out_grad, w_gate, w_up, w_down):
    all_tokens, all_grads = (
        lax.all_gather(tokens, "col", axis=0, tiled=True),
        lax.all_gather(out_grad, "col", axis=0, tiled=True),
    )
    gate_part = jnp.dot(all_tokens, w_gate, preferred_element_type=jnp.float32)
    up_part = jnp.dot(all_tokens, w_up, preferred_element_type=jnp.float32)
    grad_part = contract(all_grads, w_down, 1, 1)
    gate_sum, up_sum, hidden_grad = lax.psum((gate_part, up_part, grad_part), "row")
    hidden, gate_grad, up_grad = swiglu_back(gate_sum, up_sum, hidden_grad)
    grad_down = contract(hidden, all_grads, 0, 0).astype(jnp.bfloat16)
    grad_gate = contract(all_tokens, gate_grad, 0, 0).astype(jnp.bfloat16)
    grad_up = contract(all_tokens, up_grad, 0, 0).astype(jnp.bfloat16)
    grad_input = lax.psum_scatter(
        contract(gate_grad, w_gate, 1, 1) + contract(up_grad, w_up, 1, 1),
        "col",
        scatter_dimension=0,
        tiled=True,
    ).astype(jnp.bfloat16)
    return (grad_input, grad_gate, grad_up, grad_down)


def solution(mesh):
    return jax.shard_map(
        shards,
        mesh=mesh,
        in_specs=(
            P("col", "row"),
            P("col", "row"),
            P("row", "col"),
            P("row", "col"),
            P("col", "row"),
        ),
        out_specs=(P("col", "row"), P("row", "col"), P("row", "col"), P("col", "row")),
        check_vma=False,
    )
```

profile of v0, /device:TPU:0, one launch (start us, length us, event | category | flops | bytes accessed | tf_op | source)
XLA Modules:
  0.0 358.6 jit_solution(17293567438412855465)
XLA Ops:
  7.2 0.0 all-gather.5.cloned.1.call-start
  7.2 0.7 all-gather.5.cloned.1.call-update
  7.9 0.0 all-gather.3.cloned.1.call-start
  7.9 0.7 all-gather.3.cloned.1.call-update
  8.6 0.0 all-reduce.3.cloned.1.call-start
  8.7 27.4 %all-gather.5.cloned.1.call-done = bf16[256,2048]{1,0:T(8,128)(2,1)} async-done(((bf16[32,2048]{1,0:T(8,128)(2,1)}), bf16[256,2048]{1,0:T(8,128)(2,1)}) %all-gather.5.cloned.1.call-update) | async-done | bytes 1048592 | tf_op jit(solution)/shard_map/all_gather | solution.py:29
  36.1 0.0 copy-start
  36.1 7.4 %fusion.5 = f32[256,2048]{1,0:T(8,128)} fusion(bf16[256,2048]{1,0:T(8,128)(2,1)} %all-gather.5.cloned.1.call-done, bf16[2048,2048]{1,0:T(8,128)(2,1)} %param.7), kind=kOutput, calls=%fused_computation.12 | convolution fusion | flops 2147483648 | bytes 11534336 | tf_op jit(solution)/shard_map/dot_general | solution.py:32
  43.5 0.0 copy-done
  43.6 7.2 %fusion.4 = f32[256,2048]{1,0:T(8,128)} fusion(bf16[256,2048]{1,0:T(8,128)(2,1)S(1)} %copy-done, bf16[2048,2048]{1,0:T(8,128)(2,1)} %param.8), kind=kOutput, calls=%fused_computation.11 | convolution fusion | flops 2147483648 | bytes 11534336 | tf_op jit(solution)/shard_map/dot_general | solution.py:33
  50.7 10.8 %all-gather.3.cloned.1.call-done = bf16[256,2048]{1,0:T(8,128)(2,1)} async-done(((bf16[32,2048]{1,0:T(8,128)(2,1)}), bf16[256,2048]{1,0:T(8,128)(2,1)}) %all-gather.3.cloned.1.call-update) | async-done | bytes 1048592 | tf_op jit(solution)/shard_map/all_gather | solution.py:30
  61.5 7.4 %fusion.3 = f32[256,2048]{1,0:T(8,128)} fusion(bf16[256,2048]{1,0:T(8,128)(2,1)} %all-gather.3.cloned.1.call-done, bf16[2048,2048]{1,0:T(8,128)(2,1)} %param.9), kind=kOutput, calls=%fused_computation.10 | convolution fusion | flops 2147483648 | bytes 11534336 | tf_op jit(solution)/shard_map/dot_general | solution.py:8
  68.9 0.0 all-reduce.3.cloned.1.call-update
  68.9 0.2 reduce-scatter.2.cloned.1.call-start
  69.2 223.5 %all-reduce.3.cloned.1.call-done = (f32[256,2048]{1,0:T(8,128)}, f32[256,2048]{1,0:T(8,128)}, f32[256,2048]{1,0:T(8,128)}) async-done(((f32[256,2048]{1,0:T(8,128)}, f32[256,2048]{1,0:T(8,128)}, f32[256,2048]{1,0:T(8,128)}), (f32[256,2048]{1,0:T(8,128)}, f32[256,2048]{1,0:T(8,128)}, f32[256,2048]{1,0:T(8,128)})) %all-reduce.3.cloned.1.call-update) | async-done | bytes 6291472 | tf_op jit(solution)/shard_map/psum | solution.py:35
  292.6 4.3 %multiply_convert_fusion.1 = (bf16[256,2048]{1,0:T(8,128)(2,1)S(1)}, bf16[256,2048]{1,0:T(8,128)(2,1)S(1)}) fusion(f32[256,2048]{1,0:T(8,128)} %get-tuple-element.9, f32[256,2048]{1,0:T(8,128)} %get-tuple-element.8, f32[256,2048]{1,0:T(8,128)} %get-tuple-element.10), kind=kLoop, calls=%fused_computation.5 | loop fusion | flops 6815744 | bytes 8388608 | tf_op jit(solution)/shard_map/convert_element_type | solution.py:20
  297.0 0.0 slice-start.1
  297.0 5.9 %fusion.6 = f32[256,2048]{1,0:T(8,128)S(1)} fusion(bf16[256,2048]{1,0:T(8,128)(2,1)S(1)} %get-tuple-element.12, bf16[2048,2048]{1,0:T(8,128)(2,1)} %param.7), kind=kOutput, calls=%fused_computation.13 | convolution fusion | flops 2147483648 | bytes 11534336 | tf_op jit(solution)/shard_map/dot_general | solution.py:8
  302.9 0.0 slice-done
  302.9 0.0 slice-done.1
  302.9 3.7 %convolution_add_fusion = f32[256,2048]{1,0:T(8,128)} fusion(f32[256,2048]{1,0:T(8,128)S(1)} %fusion.6, bf16[256,2048]{1,0:T(8,128)(2,1)S(1)} %get-tuple-element.11, bf16[2048,2048]{1,0:T(8,128)(2,1)S(1)} %bitcast.20), kind=kOutput, calls=%fused_computation.3 | convolution fusion | flops 2148007936 | bytes 13631488 | tf_op jit(solution)/shard_map/dot_general | solution.py:8
  306.6 0.0 reduce-scatter.2.cloned.1.call-update
  306.6 5.8 %convert_bitcast_fusion.1 = bf16[2048,2048]{0,1:T(8,128)(2,1)} fusion(bf16[256,2048]{1,0:T(8,128)(2,1)S(1)} %get-tuple-element.12, bf16[256,2048]{1,0:T(8,128)(2,1)S(1)} %copy-done), kind=kOutput, calls=%fused_computation.1 | convolution fusion | flops 2151677952 | bytes 10485760 | tf_op jit(solution)/shard_map/dot_general | solution.py:8
  312.4 12.4 %copy.9 = bf16[2048,2048]{1,0:T(8,128)(2,1)} copy(bf16[2048,2048]{0,1:T(8,128)(2,1)} %convert_bitcast_fusion.1) | data formatting | bytes 16777216
  324.8 5.8 %convert_bitcast_fusion = bf16[2048,2048]{0,1:T(8,128)(2,1)} fusion(bf16[256,2048]{1,0:T(8,128)(2,1)S(1)} %get-tuple-element.11, bf16[256,2048]{1,0:T(8,128)(2,1)S(1)} %copy-done), kind=kOutput, calls=%fused_computation | convolution fusion | flops 2151677952 | bytes 10485760 | tf_op jit(solution)/shard_map/dot_general | solution.py:8
  330.6 0.0 copy-start.1
  330.6 0.0 copy-start.2
  330.6 12.4 %copy.10 = bf16[2048,2048]{1,0:T(8,128)(2,1)} copy(bf16[2048,2048]{0,1:T(8,128)(2,1)} %convert_bitcast_fusion) | data formatting | bytes 16777216
  343.0 0.0 copy-done.1
  343.0 0.0 copy-done.2
  343.0 7.5 %convolution_convert_fusion = bf16[2048,2048]{1,0:T(8,128)(2,1)} fusion(bf16[256,2048]{1,0:T(8,128)(2,1)S(1)} %copy-done.2, f32[256,2048]{1,0:T(8,128)} %get-tuple-element.10, f32[256,2048]{1,0:T(8,128)S(1)} %copy-done.1), kind=kOutput, calls=%fused_computation.2 | convolution fusion | flops 2154823680 | bytes 13631488 | tf_op jit(solution)/shard_map/dot_general | solution.py:8
  350.5 1.6 convert_element_type.29
  (3 shorter events, 0.0 us)
Async XLA Ops:
  7.2 28.9 %all-gather.5.cloned.1.call-start = ((), (), s32[]{:S(2)}) async-start(), calls=%async_computation.2 | async-start | bytes 1179648 | tf_op jit(solution)/shard_map/all_gather | solution.py:29
  7.9 53.6 %all-gather.3.cloned.1.call-start = ((), (), s32[]{:S(2)}) async-start(), calls=%async_computation.1 | async-start | bytes 1179648 | tf_op jit(solution)/shard_map/all_gather | solution.py:30
  8.6 284.0 %all-reduce.3.cloned.1.call-start = ((), (), s32[]{:S(2)}) async-start(), calls=%async_computation.4 | async-start | bytes 12582912 | tf_op jit(solution)/shard_map/psum | solution.py:35
  36.1 7.4 %copy-start = (bf16[256,2048]{1,0:T(8,128)(2,1)S(1)}, bf16[256,2048]{1,0:T(8,128)(2,1)}, u32[]{:S(2)}) copy-start(bf16[256,2048]{1,0:T(8,128)(2,1)} %all-gather.5.cloned.1.call-done) | copy-start | bytes 3145732
  68.9 281.5 %reduce-scatter.2.cloned.1.call-start = ((), (), s32[]{:S(2)}) async-start(), calls=%async_computation.3 | async-start | bytes 2359296 | tf_op jit(solution)/shard_map/reduce_scatter | solution.py:40
  292.6 10.2 %slice-start = ((s8[8388608]{0:T(1024)(128)(4,1)}), s8[4194304]{0:T(1024)(128)(4,1)S(1)}, s32[]{:S(2)}) async-start(s8[8388608]{0:T(1024)(128)(4,1)} %bitcast.19), calls=%async_computation.5 | async-start | bytes 8388608
  297.0 5.9 %slice-start.1 = ((s8[8388608]{0:T(1024)(128)(4,1)}), s8[4194304]{0:T(1024)(128)(4,1)S(1)}, s32[]{:S(2)}) async-start(s8[8388608]{0:T(1024)(128)(4,1)} %bitcast.19), calls=%async_computation.6 | async-start | bytes 8388608
  330.6 12.4 %copy-start.1 = (f32[256,2048]{1,0:T(8,128)S(1)}, f32[256,2048]{1,0:T(8,128)}, u32[]{:S(2)}) copy-start(f32[256,2048]{1,0:T(8,128)} %get-tuple-element.8) | copy-start | bytes 6291460
  330.6 12.4 %copy-start.2 = (bf16[256,2048]{1,0:T(8,128)(2,1)S(1)}, bf16[256,2048]{1,0:T(8,128)(2,1)}, u32[]{:S(2)}) copy-start(bf16[256,2048]{1,0:T(8,128)(2,1)} %all-gather.3.cloned.1.call-done) | copy-start | bytes 3145732
Sparse Core Ops, SparseCore 0:
  9.9 26.1 all-gather.4
  38.0 23.4 all-gather.2
  69.1 223.5 all-reduce.2
  306.8 40.1 reduce-scatter.1
where the time goes:
time: 359 us
  waiting for transfers between devices  263 us (73%)
  matrix products  50.7 us (14%)
  local copies, waits for them, and re-layouts  24.8 us (7%)
  between operations  13.8 us (4%)
  other arithmetic  5.93 us (2%)
    psum x1, waiting for transfers between devices, shards(): lax.psum((gate_part, up_part, grad_part), 'row')  223 us
    dot_general x6, matrix products, contract(): lax.dot_general(left_array, right_array, (((left_dim,), (right_dim,)), ((...  36 us
    all_gather x1, waiting for transfers between devices, shards(): lax.all_gather(tokens, 'col', axis=0, tiled=True)  27.4 us
    unnamed x12, local copies, waits for them, and re-layouts  24.8 us
    all_gather x1, waiting for transfers between devices, shards(): lax.all_gather(out_grad, 'col', axis=0, tiled=True)  10.8 us
    dot_general x1, matrix products, shards(): gate_part = jnp.dot(all_tokens, w_gate, preferred_element_type=jnp.float32)  7.44 us
  transfers between devices with their start and end apart: 4, of which 3 were waited for; matrix products, arithmetic and copies ran while one was open for 16% of the time, Pallas kernels for 0%

commit v1 on v0

--- a/solution.py
+++ b/solution.py
@@ -2,6 +2,25 @@
 import jax.numpy as jnp
 from jax import lax
 from jax.sharding import PartitionSpec as P
+
+
+def ring_gather(x, axis, dim):
+    size, mine, rows = (lax.axis_size(axis), lax.axis_index(axis), x.shape[dim])
+    right = [(i, (i + 1) % size) for i in range(size)]
+    left = [(i, (i - 1) % size) for i in range(size)]
+    out = jnp.zeros((*x.shape[:dim], size * rows, *x.shape[dim + 1 :]), x.dtype)
+    out = lax.dynamic_update_slice_in_dim(out, x, mine * rows, axis=dim)
+    from_left = from_right = x
+    halfway = size // 2
+    for turn in range(1, halfway + 1):
+        from_left = lax.ppermute(from_left, axis, right)
+        out = lax.dynamic_update_slice_in_dim(out, from_left, (mine - turn) % size * rows, axis=dim)
+        if turn < size - halfway:
+            from_right = lax.ppermute(from_right, axis, left)
+            out = lax.dynamic_update_slice_in_dim(
+                out, from_right, (mine + turn) % size * rows, axis=dim
+            )
+    return out
 
 
 def contract(left_array, right_array, left_dim, right_dim):
@@ -27,7 +46,7 @@
 def shards(tokens, out_grad, w_gate, w_up, w_down):
     all_tokens, all_grads = (
         lax.all_gather(tokens, "col", axis=0, tiled=True),
-        lax.all_gather(out_grad, "col", axis=0, tiled=True),
+        ring_gather(out_grad, "col", 0),
     )
     gate_part = jnp.dot(all_tokens, w_gate, preferred_element_type=jnp.float32)
     up_part = jnp.dot(all_tokens, w_up, preferred_element_type=jnp.float32)

time: 359 us -> 346 us (0.964)
  waiting for transfers between devices: 263 us -> 239 us
  starting transfers between devices: 0.34 us -> 9.23 us
    all_gather x1, waiting for transfers between devices: 27.4 us -> 0.01 us  [shards(): lax.all_gather(tokens, 'col', axis=0, tiled=True)]
    ppermute x0 -> x7, waiting for transfers between devices: none -> 13.5 us  [the longest x4 12.8 us: ring_gather(): from_left = lax.ppermute(from_left, axis, right)]
    all_gather x1 -> x0, waiting for transfers between devices: 10.8 us -> none  [shards(): lax.all_gather(out_grad, 'col', axis=0, tiled=True)]
    ppermute x0 -> x7, starting transfers between devices: none -> 8.93 us  [the longest x3 8.42 us: ring_gather(): from_right = lax.ppermute(from_right, axis, left)]
    unnamed x12 -> x14, local copies, waits for them, and re-layouts: 24.8 us -> 25.8 us
  transfers between devices with their start and end apart: 4 -> 10, of which waited for: 3 -> 7; matrix products, arithmetic and copies ran while one was open for 16% -> 15% of each run, Pallas kernels for 0% -> 0%
where the time goes in v1:
time: 346 us; the launch traced here: 345 us
  waiting for transfers between devices  239 us (69%)
  matrix products  50.2 us (15%)
  local copies, waits for them, and re-layouts  26.9 us (8%)
  between operations  14 us (4%)
  starting transfers between devices  9.23 us (3%)
  other arithmetic  5.93 us (2%)
    psum x1, waiting for transfers between devices, shards(): lax.psum((gate_part, up_part, grad_part), 'row')  225 us
    dot_general x6, matrix products, contract(): lax.dot_general(left_array, right_array, (((left_dim,), (right_dim,)), ((...  35.7 us
    unnamed x14, local copies, waits for them, and re-layouts  25.8 us
    ppermute x4, waiting for transfers between devices, ring_gather(): from_left = lax.ppermute(from_left, axis, right)  12.8 us
    ppermute x3, starting transfers between devices, ring_gather(): from_right = lax.ppermute(from_right, axis, left)  8.42 us
    dot_general x1, matrix products, shards(): gate_part = jnp.dot(all_tokens, w_gate, preferred_element_type=jnp.float32)  7.44 us
    dot_general x1, matrix products, shards(): up_part = jnp.dot(all_tokens, w_up, preferred_element_type=jnp.float32)  7.03 us
  transfers between devices with their start and end apart: 10, of which 7 were waited for; matrix products, arithmetic and copies ran while one was open for 15% of the time, Pallas kernels for 0%

profile of v1, /device:TPU:0, one launch (start us, length us, event | category | flops | bytes accessed | tf_op | source)
XLA Modules:
  0.0 345.1 jit_solution(4803818524556609871)
XLA Ops:
  7.2 0.0 all-gather.2.cloned.1.call-start
  7.2 0.5 collective-permute-start
  7.7 2.9 collective-permute-start.1
  10.7 0.0 all-gather.2.cloned.1.call-update
  10.7 0.0 all-reduce.3.cloned.1.call-start
  10.9 0.1 broadcast_in_dim.3
  11.0 0.9 constant_dynamic-update-slice_fusion.7
  11.9 1.5 collective-permute-done
  13.5 0.4 collective-permute-done.1
  13.8 2.7 collective-permute-start.3
  16.6 2.2 collective-permute-done.2
  18.8 0.3 collective-permute-done.3
  19.1 2.8 collective-permute-start.5
  21.9 3.9 %collective-permute-done.4 = bf16[32,2048]{1,0:T(8,128)(2,1)S(1)} collective-permute-done((bf16[32,2048]{1,0:T(8,128)(2,1)S(1)}, bf16[32,2048]{1,0:T(8,128)(2,1)S(1)}, u32[]{:S(2)}, u32[]{:S(2)}) %collective-permute-start.4) | collective-permute-done | bytes 131104 | tf_op jit(solution)/shard_map/ppermute | solution.py:16
  25.8 5.2 %collective-permute-done.6 = bf16[32,2048]{1,0:T(8,128)(2,1)S(1)} collective-permute-done((bf16[32,2048]{1,0:T(8,128)(2,1)S(1)}, bf16[32,2048]{1,0:T(8,128)(2,1)S(1)}, u32[]{:S(2)}, u32[]{:S(2)}) %collective-permute-start.6) | collective-permute-done | bytes 131104 | tf_op jit(solution)/shard_map/ppermute | solution.py:16
  31.0 1.0 copy-done.2
  32.0 7.1 %fusion.3 = f32[256,2048]{1,0:T(8,128)} fusion(bf16[256,2048]{1,0:T(8,128)(2,1)S(1)} %constant_dynamic-update-slice_fusion, bf16[2048,2048]{1,0:T(8,128)(2,1)} %param.9), kind=kOutput, calls=%fused_computation.18 | convolution fusion | flops 2147483648 | bytes 11534336 | tf_op jit(solution)/shard_map/dot_general | solution.py:27
  39.1 7.4 %fusion.5 = f32[256,2048]{1,0:T(8,128)} fusion(bf16[256,2048]{1,0:T(8,128)(2,1)} %all-gather.2.cloned.1.call-done, bf16[2048,2048]{1,0:T(8,128)(2,1)} %param.7), kind=kOutput, calls=%fused_computation.20 | convolution fusion | flops 2147483648 | bytes 11534336 | tf_op jit(solution)/shard_map/dot_general | solution.py:51
  46.5 7.0 %fusion.4 = f32[256,2048]{1,0:T(8,128)} fusion(bf16[256,2048]{1,0:T(8,128)(2,1)S(1)} %copy-done, bf16[2048,2048]{1,0:T(8,128)(2,1)} %param.8), kind=kOutput, calls=%fused_computation.19 | convolution fusion | flops 2147483648 | bytes 11534336 | tf_op jit(solution)/shard_map/dot_general | solution.py:52
  53.6 0.0 all-reduce.3.cloned.1.call-update
  53.6 0.2 reduce-scatter.2.cloned.1.call-start
  53.8 225.3 %all-reduce.3.cloned.1.call-done = (f32[256,2048]{1,0:T(8,128)}, f32[256,2048]{1,0:T(8,128)}, f32[256,2048]{1,0:T(8,128)}) async-done(((f32[256,2048]{1,0:T(8,128)}, f32[256,2048]{1,0:T(8,128)}, f32[256,2048]{1,0:T(8,128)}), (f32[256,2048]{1,0:T(8,128)}, f32[256,2048]{1,0:T(8,128)}, f32[256,2048]{1,0:T(8,128)})) %all-reduce.3.cloned.1.call-update) | async-done | bytes 6291472 | tf_op jit(solution)/shard_map/psum | solution.py:54
  279.1 4.3 %multiply_convert_fusion.1 = (bf16[256,2048]{1,0:T(8,128)(2,1)S(1)}, bf16[256,2048]{1,0:T(8,128)(2,1)S(1)}) fusion(f32[256,2048]{1,0:T(8,128)} %get-tuple-element.9, f32[256,2048]{1,0:T(8,128)} %get-tuple-element.8, f32[256,2048]{1,0:T(8,128)} %get-tuple-element.10), kind=kLoop, calls=%fused_computation.5 | loop fusion | flops 6815744 | bytes 8388608 | tf_op jit(solution)/shard_map/convert_element_type | solution.py:39
  283.5 5.9 %fusion.6 = f32[256,2048]{1,0:T(8,128)S(1)} fusion(bf16[256,2048]{1,0:T(8,128)(2,1)S(1)} %get-tuple-element.12, bf16[2048,2048]{1,0:T(8,128)(2,1)} %param.7), kind=kOutput, calls=%fused_computation.21 | convolution fusion | flops 2147483648 | bytes 11534336 | tf_op jit(solution)/shard_map/dot_general | solution.py:27
  289.4 3.7 %convolution_add_fusion = f32[256,2048]{1,0:T(8,128)} fusion(f32[256,2048]{1,0:T(8,128)S(1)} %fusion.6, bf16[256,2048]{1,0:T(8,128)(2,1)S(1)} %get-tuple-element.11, bf16[2048,2048]{1,0:T(8,128)(2,1)S(1)} %bitcast.20), kind=kOutput, calls=%fused_computation.3 | convolution fusion | flops 2148007936 | bytes 13631488 | tf_op jit(solution)/shard_map/dot_general | solution.py:27
  293.1 0.0 reduce-scatter.2.cloned.1.call-update
  293.1 5.8 %convert_bitcast_fusion.1 = bf16[2048,2048]{0,1:T(8,128)(2,1)} fusion(bf16[256,2048]{1,0:T(8,128)(2,1)S(1)} %get-tuple-element.12, bf16[256,2048]{1,0:T(8,128)(2,1)S(1)} %copy-done), kind=kOutput, calls=%fused_computation.1 | convolution fusion | flops 2151677952 | bytes 10485760 | tf_op jit(solution)/shard_map/dot_general | solution.py:27
  298.9 12.4 %copy.9 = bf16[2048,2048]{1,0:T(8,128)(2,1)} copy(bf16[2048,2048]{0,1:T(8,128)(2,1)} %convert_bitcast_fusion.1) | data formatting | bytes 16777216
  311.3 5.8 %convert_bitcast_fusion = bf16[2048,2048]{0,1:T(8,128)(2,1)} fusion(bf16[256,2048]{1,0:T(8,128)(2,1)S(1)} %get-tuple-element.11, bf16[256,2048]{1,0:T(8,128)(2,1)S(1)} %copy-done), kind=kOutput, calls=%fused_computation | convolution fusion | flops 2151677952 | bytes 10485760 | tf_op jit(solution)/shard_map/dot_general | solution.py:27
  317.1 12.4 %copy.10 = bf16[2048,2048]{1,0:T(8,128)(2,1)} copy(bf16[2048,2048]{0,1:T(8,128)(2,1)} %convert_bitcast_fusion) | data formatting | bytes 16777216
  329.5 7.5 %convolution_convert_fusion = bf16[2048,2048]{1,0:T(8,128)(2,1)} fusion(bf16[256,2048]{1,0:T(8,128)(2,1)S(1)} %copy-done.3, f32[256,2048]{1,0:T(8,128)} %get-tuple-element.10, f32[256,2048]{1,0:T(8,128)S(1)} %copy-done.1), kind=kOutput, calls=%fused_computation.2 | convolution fusion | flops 2154823680 | bytes 13631488 | tf_op jit(solution)/shard_map/dot_general | solution.py:27
  337.0 1.6 convert_element_type.29
  (25 shorter events, 0.1 us)
Async XLA Ops:
  7.2 31.9 %all-gather.2.cloned.1.call-start = ((), (), s32[]{:S(2)}) async-start(), calls=%async_computation.1 | async-start | bytes 1179648 | tf_op jit(solution)/shard_map/all_gather | solution.py:48
  7.2 6.3 %collective-permute-start = (bf16[32,2048]{1,0:T(8,128)(2,1)}, bf16[32,2048]{1,0:T(8,128)(2,1)S(1)}, u32[]{:S(2)}, u32[]{:S(2)}) collective-permute-start(bf16[32,2048]{1,0:T(8,128)(2,1)} %param.6), channel_id=1, source_target_pairs={{0,1},{1,2},{2,3},{3,4},{4,5},{5,6},{6,7},{7,0},{8,9},{9,10},{10,1... | collective-permute-start | bytes 393224 | tf_op jit(solution)/shard_map/ppermute | solution.py:16
  7.7 6.1 %collective-permute-start.1 = (bf16[32,2048]{1,0:T(8,128)(2,1)}, bf16[32,2048]{1,0:T(8,128)(2,1)S(1)}, u32[]{:S(2)}, u32[]{:S(2)}) collective-permute-start(bf16[32,2048]{1,0:T(8,128)(2,1)} %param.6), channel_id=1, source_target_pairs={{0,7},{1,0},{2,1},{3,2},{4,3},{5,4},{6,5},{7,6},{8,15},{9,8},{10,9... | collective-permute-start | bytes 393224 | tf_op jit(solution)/shard_map/ppermute | solution.py:19
  10.7 268.4 %all-reduce.3.cloned.1.call-start = ((), (), s32[]{:S(2)}) async-start(), calls=%async_computation.3 | async-start | bytes 12582912 | tf_op jit(solution)/shard_map/psum | solution.py:54
  13.5 5.3 %collective-permute-start.2 = (bf16[32,2048]{1,0:T(8,128)(2,1)S(1)}, bf16[32,2048]{1,0:T(8,128)(2,1)S(1)}, u32[]{:S(2)}, u32[]{:S(2)}) collective-permute-start(bf16[32,2048]{1,0:T(8,128)(2,1)S(1)} %collective-permute-done), channel_id=1, source_target_pairs={{0,1},{1,2},{2,3},{3,4},{4,5},{5,6},{6,7},{7,0},{8,9},{9,10},{10,1... | collective-permute-start | bytes 393224 | tf_op jit(solution)/shard_map/ppermute | solution.py:16
  13.8 5.2 %collective-permute-start.3 = (bf16[32,2048]{1,0:T(8,128)(2,1)S(1)}, bf16[32,2048]{1,0:T(8,128)(2,1)S(1)}, u32[]{:S(2)}, u32[]{:S(2)}) collective-permute-start(bf16[32,2048]{1,0:T(8,128)(2,1)S(1)} %collective-permute-done.1), channel_id=1, source_target_pairs={{0,7},{1,0},{2,1},{3,2},{4,3},{5,4},{6,5},{7,6},{8,15},{9,8},{10,9... | collective-permute-start | bytes 393224 | tf_op jit(solution)/shard_map/ppermute | solution.py:19
  18.8 7.0 %collective-permute-start.4 = (bf16[32,2048]{1,0:T(8,128)(2,1)S(1)}, bf16[32,2048]{1,0:T(8,128)(2,1)S(1)}, u32[]{:S(2)}, u32[]{:S(2)}) collective-permute-start(bf16[32,2048]{1,0:T(8,128)(2,1)S(1)} %collective-permute-done.2), channel_id=1, source_target_pairs={{0,1},{1,2},{2,3},{3,4},{4,5},{5,6},{6,7},{7,0},{8,9},{9,10},{10,1... | collective-permute-start | bytes 393224 | tf_op jit(solution)/shard_map/ppermute | solution.py:16
  19.1 6.7 %collective-permute-start.5 = (bf16[32,2048]{1,0:T(8,128)(2,1)S(1)}, bf16[32,2048]{1,0:T(8,128)(2,1)S(1)}, u32[]{:S(2)}, u32[]{:S(2)}) collective-permute-start(bf16[32,2048]{1,0:T(8,128)(2,1)S(1)} %collective-permute-done.3), channel_id=1, source_target_pairs={{0,7},{1,0},{2,1},{3,2},{4,3},{5,4},{6,5},{7,6},{8,15},{9,8},{10,9... | collective-permute-start | bytes 393224 | tf_op jit(solution)/shard_map/ppermute | solution.py:19
  25.7 5.3 %collective-permute-start.6 = (bf16[32,2048]{1,0:T(8,128)(2,1)S(1)}, bf16[32,2048]{1,0:T(8,128)(2,1)S(1)}, u32[]{:S(2)}, u32[]{:S(2)}) collective-permute-start(bf16[32,2048]{1,0:T(8,128)(2,1)S(1)} %collective-permute-done.4), channel_id=1, source_target_pairs={{0,1},{1,2},{2,3},{3,4},{4,5},{5,6},{6,7},{7,0},{8,9},{9,10},{10,1... | collective-permute-start | bytes 393224 | tf_op jit(solution)/shard_map/ppermute | solution.py:16
  31.0 1.0 copy-start.2
  39.1 7.4 %copy-start = (bf16[256,2048]{1,0:T(8,128)(2,1)S(1)}, bf16[256,2048]{1,0:T(8,128)(2,1)}, u32[]{:S(2)}) copy-start(bf16[256,2048]{1,0:T(8,128)(2,1)} %all-gather.2.cloned.1.call-done) | copy-start | bytes 3145732
  53.6 283.4 %reduce-scatter.2.cloned.1.call-start = ((), (), s32[]{:S(2)}) async-start(), calls=%async_computation.2 | async-start | bytes 2359296 | tf_op jit(solution)/shard_map/reduce_scatter | solution.py:59
  279.1 10.2 %slice-start = ((s8[8388608]{0:T(1024)(128)(4,1)}), s8[4194304]{0:T(1024)(128)(4,1)S(1)}, s32[]{:S(2)}) async-start(s8[8388608]{0:T(1024)(128)(4,1)} %bitcast.19), calls=%async_computation.4 | async-start | bytes 8388608
  283.5 5.9 %slice-start.1 = ((s8[8388608]{0:T(1024)(128)(4,1)}), s8[4194304]{0:T(1024)(128)(4,1)S(1)}, s32[]{:S(2)}) async-start(s8[8388608]{0:T(1024)(128)(4,1)} %bitcast.19), calls=%async_computation.5 | async-start | bytes 8388608
  317.1 12.4 %copy-start.1 = (f32[256,2048]{1,0:T(8,128)S(1)}, f32[256,2048]{1,0:T(8,128)}, u32[]{:S(2)}) copy-start(f32[256,2048]{1,0:T(8,128)} %get-tuple-element.8) | copy-start | bytes 6291460
  317.1 12.4 %copy-start.3 = (bf16[256,2048]{1,0:T(8,128)(2,1)S(1)}, bf16[256,2048]{1,0:T(8,128)(2,1)}, u32[]{:S(2)}) copy-start(bf16[256,2048]{1,0:T(8,128)(2,1)} %copy-done.2) | copy-start | bytes 3145732
Sparse Core Ops, SparseCore 0:
  10.8 26.4 all-gather.1
  53.7 225.3 all-reduce.2
  293.3 40.1 reduce-scatter.1
